TPU v7x, 256 devices: a whole 4x4x8 slice. The times are simulated.
256 devices in a mesh: cell: 64 (over x, z_hi, y, core), cls: 4 (over z_lo).
Axes of the slice: x: 4, y: 4, z: 8 (z_hi: 2, z_lo: 4; z = z_hi * 4 + z_lo), core: 2. Of those that a mesh axis runs over, the one named last changes fastest.
Arguments:
- melt: float32 [64, 32, 65536], P(None, 'cls', 'cell'), may hold values from 0 to 1
- counts: int32 [32, 65536], P('cls', 'cell'), may hold values from 0 to 800, as said below
- pressure: float32 [256, 256], P(('cell', 'cls')), may hold values from 0.5 to 2
- propagator: float32 [32, 64, 64], replicated, as said below
- coupling: float32 [32, 64], replicated, may hold values from 0.05 to 0.5
- flux_weights: float32 [32, 64], replicated, may hold values from 0.002 to 0.2
Outputs:
- shells_out: float32 [64, 32, 65536], P(None, 'cls', 'cell')
- pressure_out: float32 [256, 256], P(('cell', 'cls'))
Inputs may be any that keep to these rules, and one draw needn't show every extreme that they name: counts in layer l are non-negative and below 201 + (600 * l) // 255. Each propagator matrix has a dominant diagonal.
All inputs are finite; a program needn't handle non-finite values.
Results may differ from a plain program's by a relative error of at most 0.0001.
Values sent between devices are 32-bit elements; how exact they have to be, the bound alone decides.
A program may use at most 64 MiB of HBM per device.

v0:
```python
import jax
import jax.numpy as jnp
from jax import lax
from jax.sharding import PartitionSpec as P

CLASSES = 32
SIDE = 16
SUBSTEPS = 4
count_scale = 400.0


def extended_2(block, sides, width):
    for axis, dim in sides:
        count = lax.axis_size(axis)
        forward = [(i, i + 1) for i in range(count - 1)]
        backward = [(target, source) for source, target in forward]
        low = lax.ppermute(
            lax.slice_in_dim(block, block.shape[dim] - width, None, axis=dim), axis, forward
        )
        high = lax.ppermute(lax.slice_in_dim(block, 0, width, axis=dim), axis, backward)
        block = jnp.concatenate([low, block, high], axis=dim)
    return block


def shell_update(shells, counts_f, propagator, coupling, flux_weights, wall):
    shells = (
        jnp.einsum("kij,jkc->ikc", propagator, shells, precision=lax.Precision.HIGHEST)
        + coupling.T[:, :, None] * wall[None, None, :]
    )
    flux = jnp.einsum("ki,ikc->kc", flux_weights, shells, precision=lax.Precision.HIGHEST)
    partial_gas = jnp.sum(counts_f * flux, axis=0) / (count_scale * CLASSES)
    return (shells, partial_gas)


def pressure_update(tile, gas_tile):
    total = lax.psum(jnp.sum(gas_tile), ("cell", "cls"))
    all_cells = gas_tile.shape[0] * lax.axis_size("cell") * lax.axis_size("cls")
    chamber = 1.5 - 0.5 * total / all_cells
    layer_count = tile.shape[0]
    field = tile.reshape(layer_count, SIDE, SIDE)
    extended = extended_2(field, ((("cell", "cls"), 0),), 1)
    extended = jnp.pad(extended, ((0, 0), (1, 1), (1, 1)))
    lap = (
        extended[2:, 1:-1, 1:-1]
        + extended[:-2, 1:-1, 1:-1]
        + extended[1:-1, 2:, 1:-1]
        + extended[1:-1, :-2, 1:-1]
        + extended[1:-1, 1:-1, 2:]
        + extended[1:-1, 1:-1, :-2]
        - 6.0 * field
    )
    field = field + 0.15 * lap + 0.1 * gas_tile.reshape(field.shape) + 0.2 * (chamber - field)
    return field.reshape(tile.shape)


def shards(melt, counts, pressure, propagator, coupling, flux_weights):
    tile = pressure
    class_count = melt.shape[1]
    start = lax.axis_index("cls") * class_count
    local_prop = lax.dynamic_slice_in_dim(propagator, start, class_count, 0)
    local_coupling = lax.dynamic_slice_in_dim(coupling, start, class_count, 0)
    local_flux = lax.dynamic_slice_in_dim(flux_weights, start, class_count, 0)
    counts_f = counts.astype(jnp.float32)
    shells = melt
    for step in range(SUBSTEPS):
        block_pressure = lax.all_gather(tile.reshape(-1), "cls", axis=0, tiled=True)
        shells, partial_gas = shell_update(
            shells, counts_f, local_prop, local_coupling, local_flux, 0.5 * block_pressure
        )
        gas_tile = lax.psum_scatter(partial_gas, "cls", scatter_dimension=0, tiled=True)
        tile = pressure_update(tile, gas_tile)
    return (shells, tile)


def solution(mesh):
    placed = (P(None, "cls", "cell"), P("cls", "cell"), P(("cell", "cls"), None), P(), P(), P())
    return jax.shard_map(
        shards,
        mesh=mesh,
        in_specs=placed,
        out_specs=(P(None, "cls", "cell"), P(("cell", "cls"), None)),
        check_vma=False,
    )
```

profile of v0, /device:TPU:1, one launch (start us, length us, event | category | flops | bytes accessed | tf_op | source)
XLA Modules:
  0.0 445.1 jit_solution(3294544564548670002)
XLA Ops:
  0.6 0.5 broadcast.251
  1.2 1.5 reduce.3
  2.7 4.4 collective-permute-start.1
  7.1 5.2 %collective-permute-start = (f32[1,16,16]{2,1,0:T(8,128)S(1)}, f32[1,16,16]{2,1,0:T(8,128)S(1)}, u32[]{:S(2)}, u32[]{:S(2)}) collective-permute-start(f32[1,16,16]{2,1,0:T(8,128)S(1)} %reshape.107), channel_id=1, source_target_pairs={{1,0},{2,1},{3,2},{4,3},{5,4},{6,5},{7,6},{8,7},{9,8},{10,9},{11,1... | collective-permute-start | bytes 3080 | tf_op jit(solution)/shard_map/ppermute | solution.py:20
  12.3 7.0 %all-gather = f32[1,1024]{1,0:T(1,128)S(1)} all-gather(f32[1,256]{1,0:T(1,128)} %param.8), channel_id=2, replica_groups=mesh['cell'=64,'cls'=4] {'cls'}, dimensions={1}, use_global_device_ids=true | all-gather | bytes 5120 | tf_op jit(solution)/shard_map/all_gather | solution.py:66
  19.2 1.3 dynamic-slice
  21.2 0.7 dynamic-slice_bitcast_fusion
  21.9 4.0 fusion
  25.9 1.3 copy-done.1
  27.2 1.3 fusion.2
  28.6 7.5 %all-reduce.4 = f32[1024]{0:T(1024)S(1)} all-reduce(f32[1024]{0:T(1024)S(1)} %broadcast_multiply_fusion.7), channel_id=3, replica_groups=mesh['cell'=64,'cls'=4] {'cls'}, use_global_device_ids=true, to_apply=%region_1.0.clone | all-reduce | flops 1024 | bytes 8192
  36.1 0.7 dynamic-slice_reduce_fusion.3
  36.7 80.6 %psum.28 = f32[]{:T(128)} all-reduce(f32[]{:T(128)} %get-tuple-element.12), channel_id=1, replica_groups=mesh['cell'=64,'cls'=4] {'cell','cls'}, use_global_device_ids=true, to_apply=%region_3.0 | all-reduce | flops 1 | bytes 8 | tf_op jit(solution)/shard_map/psum | solution.py:36
  118.1 0.1 select_maximum_fusion.6
  118.2 0.1 fusion.45
  118.3 3.5 collective-permute-start.3
  121.8 4.4 collective-permute-start.2
  126.2 6.7 %all-gather.1 = f32[4,1,256]{2,1,0:T(1,128)S(1)} all-gather(f32[1,1,256]{2,1,0:T(1,128)S(1)} %reshape.112), channel_id=1, replica_groups=mesh['cell'=64,'cls'=4] {'cls'}, dimensions={0}, use_global_device_ids=true | all-gather | bytes 5120 | tf_op jit(solution)/shard_map/all_gather | solution.py:66
  132.9 3.9 bitcast_add_fusion.2
  136.9 1.1 fusion.50
  138.0 3.3 fusion.15
  141.3 7.5 %all-reduce.5 = f32[1024]{0:T(1024)S(1)} all-reduce(f32[1024]{0:T(1024)S(1)} %broadcast_multiply_fusion.6), channel_id=4, replica_groups=mesh['cell'=64,'cls'=4] {'cls'}, use_global_device_ids=true, to_apply=%region_5.6.clone | all-reduce | flops 1024 | bytes 8192
  148.8 0.7 dynamic-slice_reduce_fusion.2
  149.5 78.4 %psum.29 = f32[]{:T(128)} all-reduce(f32[]{:T(128)} %get-tuple-element.10), channel_id=1, replica_groups=mesh['cell'=64,'cls'=4] {'cell','cls'}, use_global_device_ids=true, to_apply=%region_7.8 | all-reduce | flops 1 | bytes 8 | tf_op jit(solution)/shard_map/psum | solution.py:36
  228.6 0.1 select_maximum_fusion.4
  228.7 0.1 fusion.40
  228.9 3.7 collective-permute-start.5
  232.6 3.8 collective-permute-start.4
  236.4 6.5 %all-gather.2 = f32[4,1,256]{2,1,0:T(1,128)S(1)} all-gather(f32[1,1,256]{2,1,0:T(1,128)S(1)} %reshape.114), channel_id=1, replica_groups=mesh['cell'=64,'cls'=4] {'cls'}, dimensions={0}, use_global_device_ids=true | all-gather | bytes 5120 | tf_op jit(solution)/shard_map/all_gather | solution.py:66
  242.8 2.9 fusion.4
  245.8 7.8 %all-reduce.6 = f32[1024]{0:T(1024)S(1)} all-reduce(f32[1024]{0:T(1024)S(1)} %broadcast_multiply_fusion.5), channel_id=5, replica_groups=mesh['cell'=64,'cls'=4] {'cls'}, use_global_device_ids=true, to_apply=%region_9.10.clone | all-reduce | flops 1024 | bytes 8192
  253.5 0.7 dynamic-slice_reduce_fusion.1
  254.2 77.2 %psum.30 = f32[]{:T(128)} all-reduce(f32[]{:T(128)} %get-tuple-element.8), channel_id=1, replica_groups=mesh['cell'=64,'cls'=4] {'cell','cls'}, use_global_device_ids=true, to_apply=%region_11.12 | all-reduce | flops 1 | bytes 8 | tf_op jit(solution)/shard_map/psum | solution.py:36
  332.2 0.1 select_maximum_fusion.2
  332.3 0.1 fusion.35
  332.4 3.7 collective-permute-start.7
  336.1 3.7 collective-permute-start.6
  339.8 6.1 %all-gather.3 = f32[4,1,256]{2,1,0:T(1,128)S(1)} all-gather(f32[1,1,256]{2,1,0:T(1,128)S(1)} %reshape.116), channel_id=1, replica_groups=mesh['cell'=64,'cls'=4] {'cls'}, dimensions={0}, use_global_device_ids=true | all-gather | bytes 5120 | tf_op jit(solution)/shard_map/all_gather | solution.py:66
  345.9 3.9 bitcast_add_fusion
  349.9 1.3 copy-done.2
  351.2 1.1 fusion.51
  352.3 8.0 %all-reduce.7 = f32[1024]{0:T(1024)S(1)} all-reduce(f32[1024]{0:T(1024)S(1)} %broadcast_multiply_fusion.4), channel_id=6, replica_groups=mesh['cell'=64,'cls'=4] {'cls'}, use_global_device_ids=true, to_apply=%region_13.14.clone | all-reduce | flops 1024 | bytes 8192
  360.3 0.7 dynamic-slice_reduce_fusion
  361.0 78.4 %psum.31 = f32[]{:T(128)} all-reduce(f32[]{:T(128)} %get-tuple-element.6), channel_id=1, replica_groups=mesh['cell'=64,'cls'=4] {'cell','cls'}, use_global_device_ids=true, to_apply=%region_15.16 | all-reduce | flops 1 | bytes 8 | tf_op jit(solution)/shard_map/psum | solution.py:36
  439.4 4.1 copy.11
  444.3 0.1 select_maximum_fusion
  444.4 0.1 fusion.30
  444.4 0.6 reshape.108
  (36 shorter events, 0.8 us)
Async XLA Ops:
  0.6 21.2 %copy-start = (f32[64,8,1024]{2,1,0:T(8,128)S(1)}, f32[64,8,1024]{2,1,0:T(8,128)}, u32[]{:S(2)}) copy-start(f32[64,8,1024]{2,1,0:T(8,128)} %param.6) | copy-start | bytes 6291460
  2.7 115.4 %collective-permute-start.1 = (f32[1,16,16]{2,1,0:T(8,128)S(1)}, f32[1,16,16]{2,1,0:T(8,128)S(1)}, u32[]{:S(2)}, u32[]{:S(2)}) collective-permute-start(f32[1,16,16]{2,1,0:T(8,128)S(1)} %reshape.107), channel_id=1, source_target_pairs={{0,1},{1,2},{2,3},{3,4},{4,5},{5,6},{6,7},{7,8},{8,9},{9,10},{10,1... | collective-permute-start | bytes 3080 | tf_op jit(solution)/shard_map/ppermute | solution.py:17
  7.1 111.0 %collective-permute-start = (f32[1,16,16]{2,1,0:T(8,128)S(1)}, f32[1,16,16]{2,1,0:T(8,128)S(1)}, u32[]{:S(2)}, u32[]{:S(2)}) collective-permute-start(f32[1,16,16]{2,1,0:T(8,128)S(1)} %reshape.107), channel_id=1, source_target_pairs={{1,0},{2,1},{3,2},{4,3},{5,4},{6,5},{7,6},{8,7},{9,8},{10,9},{11,1... | collective-permute-start | bytes 3080 | tf_op jit(solution)/shard_map/ppermute | solution.py:20
  25.9 1.3 copy-start.1
  25.9 2.6 copy-start.4
  25.9 107.0 %copy-start.3 = (f32[32,64,64]{2,1,0:T(8,128)S(1)}, f32[32,64,64]{2,1,0:T(8,128)}, u32[]{:S(2)}) copy-start(f32[32,64,64]{2,1,0:T(8,128)} %param.9) | copy-start | bytes 1572868
  118.3 110.3 %collective-permute-start.3 = (f32[1,16,16]{2,1,0:T(8,128)S(1)}, f32[1,16,16]{2,1,0:T(8,128)S(1)}, u32[]{:S(2)}, u32[]{:S(2)}) collective-permute-start(f32[1,16,16]{2,1,0:T(8,128)S(1)} %fusion.45), channel_id=1, source_target_pairs={{0,1},{1,2},{2,3},{3,4},{4,5},{5,6},{6,7},{7,8},{8,9},{9,10},{10,1... | collective-permute-start | bytes 3080 | tf_op jit(solution)/shard_map/ppermute | solution.py:17
  121.8 106.8 %collective-permute-start.2 = (f32[1,16,16]{2,1,0:T(8,128)S(1)}, f32[1,16,16]{2,1,0:T(8,128)S(1)}, u32[]{:S(2)}, u32[]{:S(2)}) collective-permute-start(f32[1,16,16]{2,1,0:T(8,128)S(1)} %fusion.45), channel_id=1, source_target_pairs={{1,0},{2,1},{3,2},{4,3},{5,4},{6,5},{7,6},{8,7},{9,8},{10,9},{11,1... | collective-permute-start | bytes 3080 | tf_op jit(solution)/shard_map/ppermute | solution.py:20
  228.9 103.3 %collective-permute-start.5 = (f32[1,16,16]{2,1,0:T(8,128)S(1)}, f32[1,16,16]{2,1,0:T(8,128)S(1)}, u32[]{:S(2)}, u32[]{:S(2)}) collective-permute-start(f32[1,16,16]{2,1,0:T(8,128)S(1)} %fusion.40), channel_id=1, source_target_pairs={{0,1},{1,2},{2,3},{3,4},{4,5},{5,6},{6,7},{7,8},{8,9},{9,10},{10,1... | collective-permute-start | bytes 3080 | tf_op jit(solution)/shard_map/ppermute | solution.py:17
  232.6 99.6 %collective-permute-start.4 = (f32[1,16,16]{2,1,0:T(8,128)S(1)}, f32[1,16,16]{2,1,0:T(8,128)S(1)}, u32[]{:S(2)}, u32[]{:S(2)}) collective-permute-start(f32[1,16,16]{2,1,0:T(8,128)S(1)} %fusion.40), channel_id=1, source_target_pairs={{1,0},{2,1},{3,2},{4,3},{5,4},{6,5},{7,6},{8,7},{9,8},{10,9},{11,1... | collective-permute-start | bytes 3080 | tf_op jit(solution)/shard_map/ppermute | solution.py:20
  332.4 111.8 %collective-permute-start.7 = (f32[1,16,16]{2,1,0:T(8,128)S(1)}, f32[1,16,16]{2,1,0:T(8,128)S(1)}, u32[]{:S(2)}, u32[]{:S(2)}) collective-permute-start(f32[1,16,16]{2,1,0:T(8,128)S(1)} %fusion.35), channel_id=1, source_target_pairs={{0,1},{1,2},{2,3},{3,4},{4,5},{5,6},{6,7},{7,8},{8,9},{9,10},{10,1... | collective-permute-start | bytes 3080 | tf_op jit(solution)/shard_map/ppermute | solution.py:17
  336.1 108.2 %collective-permute-start.6 = (f32[1,16,16]{2,1,0:T(8,128)S(1)}, f32[1,16,16]{2,1,0:T(8,128)S(1)}, u32[]{:S(2)}, u32[]{:S(2)}) collective-permute-start(f32[1,16,16]{2,1,0:T(8,128)S(1)} %fusion.35), channel_id=1, source_target_pairs={{1,0},{2,1},{3,2},{4,3},{5,4},{6,5},{7,6},{8,7},{9,8},{10,9},{11,1... | collective-permute-start | bytes 3080 | tf_op jit(solution)/shard_map/ppermute | solution.py:20
  349.9 1.4 copy-start.2
where the time goes:
time: 446 us; the launch traced here: 445 us
  blocking collectives  372 us (83%)
  starting transfers between devices  32.2 us (7%)
  matrix products  21.6 us (5%)
  local copies, waits for them, and re-layouts  10.6 us (2%)
  other arithmetic  4.92 us (1%)
    psum x4, blocking collectives, pressure_update(): total = lax.psum(jnp.sum(gas_tile), ('cell', 'cls'))  315 us
    unnamed x4, blocking collectives  30.7 us
    all_gather x4, blocking collectives, shards(): block_pressure = lax.all_gather(tile.reshape(-1), 'cls', axis=0, tiled=True)  26.3 us
    ppermute x4, starting transfers between devices, extended_2(): lax.ppermute(lax.slice_in_dim(block, 0, width, axis=dim), axis, backward)  17 us
    ppermute x4, starting transfers between devices, extended_2(): lax.ppermute(lax.slice_in_dim(block, block.shape[dim] - width, None, axis...  15.2 us
    dot_general x4, matrix products, shell_update(): jnp.einsum('kij,jkc->ikc', propagator, shells, precision=lax.Precision.HI...  15.2 us
  transfers between devices with their start and end apart: 8, of which 0 were waited for; matrix products, arithmetic and copies ran while one was open for 7% of the time, Pallas kernels for 0%

commit v1 on v0

--- a/solution.py
+++ b/solution.py
@@ -63,7 +63,11 @@
     counts_f = counts.astype(jnp.float32)
     shells = melt
     for step in range(SUBSTEPS):
-        block_pressure = lax.all_gather(tile.reshape(-1), "cls", axis=0, tiled=True)
+        x = tile.reshape(-1)
+        size = lax.axis_size("cls")
+        blocks = jnp.stack([x for _ in range(size)])
+        blocks = lax.all_to_all(blocks, "cls", split_axis=0, concat_axis=0)
+        block_pressure = jnp.concatenate(blocks, axis=0)
         shells, partial_gas = shell_update(
             shells, counts_f, local_prop, local_coupling, local_flux, 0.5 * block_pressure
         )

time: 446 us -> 449 us (level)
  blocking collectives: 372 us -> 344 us
  starting transfers between devices: 32.2 us -> 45.5 us
  waiting for transfers between devices: 0.02 us -> 12.9 us
    all_gather x4 -> x0, blocking collectives: 26.3 us -> none  [shards(): block_pressure = lax.all_gather(tile.reshape(-1), 'cls', axis=0, tiled=True)]
    all_to_all x0 -> x4, starting transfers between devices: none -> 13 us  [shards(): blocks = lax.all_to_all(blocks, 'cls', split_axis=0, concat_axis=0)]
    all_to_all x0 -> x4, waiting for transfers between devices: none -> 12.9 us  [shards(): blocks = lax.all_to_all(blocks, 'cls', split_axis=0, concat_axis=0)]
  transfers between devices with their start and end apart: 8 -> 12, of which waited for: 0 -> 3; matrix products, arithmetic and copies ran while one was open for 7% -> 3% of each run, Pallas kernels for 0% -> 0%
where the time goes in v1:
time: 449 us; the launch traced here: 447 us
  blocking collectives  344 us (77%)
  starting transfers between devices  45.5 us (10%)
  matrix products  26 us (6%)
  waiting for transfers between devices  12.9 us (3%)
  local copies, waits for them, and re-layouts  10.1 us (2%)
  other arithmetic  4.92 us (1%)
    psum x4, blocking collectives, pressure_update(): total = lax.psum(jnp.sum(gas_tile), ('cell', 'cls'))  312 us
    unnamed x4, blocking collectives  31.7 us
    ppermute x4, starting transfers between devices, extended_2(): lax.ppermute(lax.slice_in_dim(block, 0, width, axis=dim), axis, backward)  18.2 us
    dot_general x4, matrix products, shell_update(): jnp.einsum('kij,jkc->ikc', propagator, shells, precision=lax.Precision.HI...  18 us
    ppermute x4, starting transfers between devices, extended_2(): lax.ppermute(lax.slice_in_dim(block, block.shape[dim] - width, None, axis...  14.3 us
    all_to_all x4, starting transfers between devices, shards(): blocks = lax.all_to_all(blocks, 'cls', split_axis=0, concat_axis=0)  13 us
    all_to_all x4, waiting for transfers between devices, shards(): blocks = lax.all_to_all(blocks, 'cls', split_axis=0, concat_axis=0)  12.9 us
  transfers between devices with their start and end apart: 12, of which 3 were waited for; matrix products, arithmetic and copies ran while one was open for 3% of the time, Pallas kernels for 0%

profile of v1, /device:TPU:1, one launch (start us, length us, event | category | flops | bytes accessed | tf_op | source)
XLA Modules:
  0.0 447.2 jit_solution(18333821294041551090)
XLA Ops:
  0.6 0.5 broadcast.279
  1.2 1.5 reduce.3
  2.7 4.4 collective-permute-start.1
  7.1 5.2 %collective-permute-start = (f32[1,16,16]{2,1,0:T(8,128)S(1)}, f32[1,16,16]{2,1,0:T(8,128)S(1)}, u32[]{:S(2)}, u32[]{:S(2)}) collective-permute-start(f32[1,16,16]{2,1,0:T(8,128)S(1)} %reshape.169), channel_id=1, source_target_pairs={{1,0},{2,1},{3,2},{4,3},{5,4},{6,5},{7,6},{8,7},{9,8},{10,9},{11,1... | collective-permute-start | bytes 3080 | tf_op jit(solution)/shard_map/ppermute | solution.py:20
  12.2 1.3 stack.18
  13.5 3.2 all-to-all-start
  16.8 5.3 %fusion = f32[8,64,1024]{2,1,0:T(8,128)} fusion(f32[64,8,1024]{2,1,0:T(8,128)S(1)} %copy-done, f32[32,64,64]{2,1,0:T(8,128)} %param.9, s32[]{:T(128)S(6)} %select_n.2), kind=kOutput, calls=%fused_computation.4 | convolution fusion | flops 402653184 | bytes 4456452 | tf_op jit(solution)/shard_map/kij,jkc->ikc/dot_general | solution.py:27
  22.1 0.8 dynamic-slice_bitcast_fusion
  22.9 0.6 dynamic-slice
  24.2 0.1 select_maximum_fusion.6
  24.3 2.9 fusion.2
  27.2 9.9 %all-reduce.4 = f32[1024]{0:T(1024)S(1)} all-reduce(f32[1024]{0:T(1024)S(1)} %broadcast_multiply_fusion.3), channel_id=2, replica_groups=mesh['cell'=64,'cls'=4] {'cls'}, use_global_device_ids=true, to_apply=%region_1.0.clone | all-reduce | flops 1024 | bytes 8192
  37.1 0.7 dynamic-slice_reduce_fusion.3
  37.8 78.9 %psum.28 = f32[]{:T(128)} all-reduce(f32[]{:T(128)} %get-tuple-element.12), channel_id=1, replica_groups=mesh['cell'=64,'cls'=4] {'cell','cls'}, use_global_device_ids=true, to_apply=%region_3.0 | all-reduce | flops 1 | bytes 8 | tf_op jit(solution)/shard_map/psum | solution.py:36
  117.5 3.7 collective-permute-start.3
  121.2 4.4 collective-permute-start.2
  125.6 0.6 stack.20
  126.2 3.2 all-to-all-start.1
  129.5 0.1 select_maximum_fusion.4
  129.6 4.3 all-to-all-done.1
  133.9 3.9 bitcast_add_fusion.2
  137.8 1.3 copy-done.1
  139.2 1.1 fusion.50
  140.3 7.2 %all-reduce.5 = f32[1024]{0:T(1024)S(1)} all-reduce(f32[1024]{0:T(1024)S(1)} %broadcast_multiply_fusion.2), channel_id=3, replica_groups=mesh['cell'=64,'cls'=4] {'cls'}, use_global_device_ids=true, to_apply=%region_5.6.clone | all-reduce | flops 1024 | bytes 8192
  147.5 0.7 dynamic-slice_reduce_fusion.2
  148.2 78.1 %psum.29 = f32[]{:T(128)} all-reduce(f32[]{:T(128)} %get-tuple-element.10), channel_id=1, replica_groups=mesh['cell'=64,'cls'=4] {'cell','cls'}, use_global_device_ids=true, to_apply=%region_7.8 | all-reduce | flops 1 | bytes 8 | tf_op jit(solution)/shard_map/psum | solution.py:36
  227.1 2.7 collective-permute-start.5
  229.7 4.9 %collective-permute-start.4 = (f32[1,16,16]{2,1,0:T(8,128)S(1)}, f32[1,16,16]{2,1,0:T(8,128)S(1)}, u32[]{:S(2)}, u32[]{:S(2)}) collective-permute-start(f32[1,16,16]{2,1,0:T(8,128)S(1)} %fusion.40), channel_id=1, source_target_pairs={{1,0},{2,1},{3,2},{4,3},{5,4},{6,5},{7,6},{8,7},{9,8},{10,9},{11,1... | collective-permute-start | bytes 3080 | tf_op jit(solution)/shard_map/ppermute | solution.py:20
  234.6 4.9 %fusion.15 = f32[8,1024,64]{1,2,0:T(8,128)} fusion(f32[64,8,1024]{2,0,1:T(8,128)} %copy-done.1, f32[32,64,64]{2,1,0:T(8,128)S(1)} %copy-done.2, s32[]{:T(128)S(6)} %select_n.2), kind=kOutput, calls=%fused_computation.19 | convolution fusion | flops 402653184 | bytes 4456452 | tf_op jit(solution)/shard_map/kij,jkc->ikc/dot_general | solution.py:27
  239.6 0.6 stack.22
  240.2 3.2 all-to-all-start.2
  243.5 4.3 all-to-all-done.2
  247.8 2.9 fusion.4
  250.8 7.4 %all-reduce.6 = f32[1024]{0:T(1024)S(1)} all-reduce(f32[1024]{0:T(1024)S(1)} %broadcast_multiply_fusion.1), channel_id=4, replica_groups=mesh['cell'=64,'cls'=4] {'cls'}, use_global_device_ids=true, to_apply=%region_9.10.clone | all-reduce | flops 1024 | bytes 8192
  258.1 0.7 dynamic-slice_reduce_fusion.1
  258.8 77.3 %psum.30 = f32[]{:T(128)} all-reduce(f32[]{:T(128)} %get-tuple-element.8), channel_id=1, replica_groups=mesh['cell'=64,'cls'=4] {'cell','cls'}, use_global_device_ids=true, to_apply=%region_11.12 | all-reduce | flops 1 | bytes 8 | tf_op jit(solution)/shard_map/psum | solution.py:36
  336.9 3.6 collective-permute-start.7
  340.6 3.7 collective-permute-start.6
  344.4 0.6 stack.24
  345.0 3.2 all-to-all-start.3
  348.3 4.3 all-to-all-done.3
  352.6 3.9 bitcast_add_fusion
  356.5 1.1 fusion.51
  357.6 2.5 copy.11
  360.2 7.2 %all-reduce.7 = f32[1024]{0:T(1024)S(1)} all-reduce(f32[1024]{0:T(1024)S(1)} %broadcast_multiply_fusion), channel_id=5, replica_groups=mesh['cell'=64,'cls'=4] {'cls'}, use_global_device_ids=true, to_apply=%region_13.14.clone | all-reduce | flops 1024 | bytes 8192
  367.4 0.7 dynamic-slice_reduce_fusion
  368.1 77.6 %psum.31 = f32[]{:T(128)} all-reduce(f32[]{:T(128)} %get-tuple-element.6), channel_id=1, replica_groups=mesh['cell'=64,'cls'=4] {'cell','cls'}, use_global_device_ids=true, to_apply=%region_15.16 | all-reduce | flops 1 | bytes 8 | tf_op jit(solution)/shard_map/psum | solution.py:36
  446.5 0.7 reshape.170
  (44 shorter events, 1.3 us)
Async XLA Ops:
  0.6 16.2 %copy-start = (f32[64,8,1024]{2,1,0:T(8,128)S(1)}, f32[64,8,1024]{2,1,0:T(8,128)}, u32[]{:S(2)}) copy-start(f32[64,8,1024]{2,1,0:T(8,128)} %param.6) | copy-start | bytes 6291460
  2.7 21.5 %collective-permute-start.1 = (f32[1,16,16]{2,1,0:T(8,128)S(1)}, f32[1,16,16]{2,1,0:T(8,128)S(1)}, u32[]{:S(2)}, u32[]{:S(2)}) collective-permute-start(f32[1,16,16]{2,1,0:T(8,128)S(1)} %reshape.169), channel_id=1, source_target_pairs={{0,1},{1,2},{2,3},{3,4},{4,5},{5,6},{6,7},{7,8},{8,9},{9,10},{10,1... | collective-permute-start | bytes 3080 | tf_op jit(solution)/shard_map/ppermute | solution.py:17
  7.1 17.1 %collective-permute-start = (f32[1,16,16]{2,1,0:T(8,128)S(1)}, f32[1,16,16]{2,1,0:T(8,128)S(1)}, u32[]{:S(2)}, u32[]{:S(2)}) collective-permute-start(f32[1,16,16]{2,1,0:T(8,128)S(1)} %reshape.169), channel_id=1, source_target_pairs={{1,0},{2,1},{3,2},{4,3},{5,4},{6,5},{7,6},{8,7},{9,8},{10,9},{11,1... | collective-permute-start | bytes 3080 | tf_op jit(solution)/shard_map/ppermute | solution.py:20
  13.5 10.7 %all-to-all-start = ((f32[4,1,256]{2,1,0:T(1,128)}), f32[4,1,256]{2,1,0:T(1,128)S(1)}, u32[]{:S(2)}, u32[]{:S(2)}) async-start(f32[4,1,256]{2,1,0:T(1,128)} %stack.18), calls=%async_computation | async-start | bytes 8192 | tf_op jit(solution)/shard_map/all_to_all | solution.py:69
  16.8 6.1 %copy-start.4 = (u32[256]{0:T(256)S(1)}, u32[256]{0:T(256)}, u32[]{:S(2)}) copy-start(u32[256]{0:T(256)} %constant.53) | copy-start | bytes 3076
  22.1 5.1 %copy-start.3 = (s32[8,1024]{1,0:T(8,128)S(1)}, s32[8,1024]{1,0:T(8,128)}, u32[]{:S(2)}) copy-start(s32[8,1024]{1,0:T(8,128)} %param.7) | copy-start | bytes 98308
  22.1 111.8 %copy-start.2 = (f32[32,64,64]{2,1,0:T(8,128)S(1)}, f32[32,64,64]{2,1,0:T(8,128)}, u32[]{:S(2)}) copy-start(f32[32,64,64]{2,1,0:T(8,128)} %param.9) | copy-start | bytes 1572868
  117.5 12.0 %collective-permute-start.3 = (f32[1,16,16]{2,1,0:T(8,128)S(1)}, f32[1,16,16]{2,1,0:T(8,128)S(1)}, u32[]{:S(2)}, u32[]{:S(2)}) collective-permute-start(f32[1,16,16]{2,1,0:T(8,128)S(1)} %fusion.45), channel_id=1, source_target_pairs={{0,1},{1,2},{2,3},{3,4},{4,5},{5,6},{6,7},{7,8},{8,9},{9,10},{10,1... | collective-permute-start | bytes 3080 | tf_op jit(solution)/shard_map/ppermute | solution.py:17
  121.2 8.3 %collective-permute-start.2 = (f32[1,16,16]{2,1,0:T(8,128)S(1)}, f32[1,16,16]{2,1,0:T(8,128)S(1)}, u32[]{:S(2)}, u32[]{:S(2)}) collective-permute-start(f32[1,16,16]{2,1,0:T(8,128)S(1)} %fusion.45), channel_id=1, source_target_pairs={{1,0},{2,1},{3,2},{4,3},{5,4},{6,5},{7,6},{8,7},{9,8},{10,9},{11,1... | collective-permute-start | bytes 3080 | tf_op jit(solution)/shard_map/ppermute | solution.py:20
  126.2 7.6 %all-to-all-start.1 = ((f32[4,1,256]{2,1,0:T(1,128)}), f32[4,1,256]{2,1,0:T(1,128)S(1)}, u32[]{:S(2)}, u32[]{:S(2)}) async-start(f32[4,1,256]{2,1,0:T(1,128)} %stack.20), calls=%async_computation.1 | async-start | bytes 8192 | tf_op jit(solution)/shard_map/all_to_all | solution.py:69
  137.8 1.3 copy-start.1
  227.1 16.4 %collective-permute-start.5 = (f32[1,16,16]{2,1,0:T(8,128)S(1)}, f32[1,16,16]{2,1,0:T(8,128)S(1)}, u32[]{:S(2)}, u32[]{:S(2)}) collective-permute-start(f32[1,16,16]{2,1,0:T(8,128)S(1)} %fusion.40), channel_id=1, source_target_pairs={{0,1},{1,2},{2,3},{3,4},{4,5},{5,6},{6,7},{7,8},{8,9},{9,10},{10,1... | collective-permute-start | bytes 3080 | tf_op jit(solution)/shard_map/ppermute | solution.py:17
  229.7 13.7 %collective-permute-start.4 = (f32[1,16,16]{2,1,0:T(8,128)S(1)}, f32[1,16,16]{2,1,0:T(8,128)S(1)}, u32[]{:S(2)}, u32[]{:S(2)}) collective-permute-start(f32[1,16,16]{2,1,0:T(8,128)S(1)} %fusion.40), channel_id=1, source_target_pairs={{1,0},{2,1},{3,2},{4,3},{5,4},{6,5},{7,6},{8,7},{9,8},{10,9},{11,1... | collective-permute-start | bytes 3080 | tf_op jit(solution)/shard_map/ppermute | solution.py:20
  240.2 7.7 %all-to-all-start.2 = ((f32[4,1,256]{2,1,0:T(1,128)}), f32[4,1,256]{2,1,0:T(1,128)S(1)}, u32[]{:S(2)}, u32[]{:S(2)}) async-start(f32[4,1,256]{2,1,0:T(1,128)} %stack.22), calls=%async_computation.2 | async-start | bytes 8192 | tf_op jit(solution)/shard_map/all_to_all | solution.py:69
  336.9 11.3 %collective-permute-start.7 = (f32[1,16,16]{2,1,0:T(8,128)S(1)}, f32[1,16,16]{2,1,0:T(8,128)S(1)}, u32[]{:S(2)}, u32[]{:S(2)}) collective-permute-start(f32[1,16,16]{2,1,0:T(8,128)S(1)} %fusion.35), channel_id=1, source_target_pairs={{0,1},{1,2},{2,3},{3,4},{4,5},{5,6},{6,7},{7,8},{8,9},{9,10},{10,1... | collective-permute-start | bytes 3080 | tf_op jit(solution)/shard_map/ppermute | solution.py:17
  340.6 7.7 %collective-permute-start.6 = (f32[1,16,16]{2,1,0:T(8,128)S(1)}, f32[1,16,16]{2,1,0:T(8,128)S(1)}, u32[]{:S(2)}, u32[]{:S(2)}) collective-permute-start(f32[1,16,16]{2,1,0:T(8,128)S(1)} %fusion.35), channel_id=1, source_target_pairs={{1,0},{2,1},{3,2},{4,3},{5,4},{6,5},{7,6},{8,7},{9,8},{10,9},{11,1... | collective-permute-start | bytes 3080 | tf_op jit(solution)/shard_map/ppermute | solution.py:20
  345.0 7.7 %all-to-all-start.3 = ((f32[4,1,256]{2,1,0:T(1,128)}), f32[4,1,256]{2,1,0:T(1,128)S(1)}, u32[]{:S(2)}, u32[]{:S(2)}) async-start(f32[4,1,256]{2,1,0:T(1,128)} %stack.24), calls=%async_computation.3 | async-start | bytes 8192 | tf_op jit(solution)/shard_map/all_to_all | solution.py:69
